TPU v7x, 32 devices: a whole 2x2x4 slice. The times are simulated.
32 devices in a mesh: dp: 16 (over z, y, core), fsdp: 2 (over x).
Axes of the slice: x: 2, y: 2, z: 4, core: 2. Of those that a mesh axis runs over, the one named last changes fastest.
Arguments:
- hidden_in: bfloat16 [4096, 1024], P(('dp', 'fsdp')), may hold values from -6 to 6
- doc_id: int32 [4096], P(('dp', 'fsdp')), may hold values from 0 to 128, as said below
- expert_ids: int32 [4096, 8], P(('dp', 'fsdp')), may hold values from 0 to 15, all different within a row
- out_grad: bfloat16 [4096, 1024], P(('dp', 'fsdp')), may hold values from -6 to 6
- attn_gain: bfloat16 [1024], P(('dp', 'fsdp')), may hold values from 0.5 to 1.5
- query_weight: bfloat16 [1024, 1024], P(('dp', 'fsdp')), may hold values from -0.1875 to 0.1875
- key_weight: bfloat16 [1024, 512], P(('dp', 'fsdp')), may hold values from -0.1875 to 0.1875
- value_weight: bfloat16 [1024, 512], P(('dp', 'fsdp')), may hold values from -0.1875 to 0.1875
- output_weight: bfloat16 [1024, 1024], P(('dp', 'fsdp')), may hold values from -0.75 to 0.75
- ffn_gain: bfloat16 [1024], P(('dp', 'fsdp')), may hold values from 0.5 to 1.5
- router_weight: bfloat16 [1024, 16], P(('dp', 'fsdp')), may hold values from -0.375 to 0.375
- expert_gate: bfloat16 [16, 1024, 512], P('dp', 'fsdp'), may hold values from -0.1875 to 0.1875
- expert_up: bfloat16 [16, 1024, 512], P('dp', 'fsdp'), may hold values from -0.1875 to 0.1875
- expert_down: bfloat16 [16, 512, 1024], P('dp', 'fsdp'), may hold values from -1 to 1
Outputs:
- layer_out: bfloat16 [4096, 1024], P(('dp', 'fsdp'))
- grad_in: bfloat16 [4096, 1024], P(('dp', 'fsdp'))
- grad_attn_gain: float32 [1024], P(('dp', 'fsdp'))
- grad_query: float32 [1024, 1024], P(('dp', 'fsdp'))
- grad_key: float32 [1024, 512], P(('dp', 'fsdp'))
- grad_value: float32 [1024, 512], P(('dp', 'fsdp'))
- grad_output: float32 [1024, 1024], P(('dp', 'fsdp'))
- grad_ffn_gain: float32 [1024], P(('dp', 'fsdp'))
- grad_router: float32 [1024, 16], P(('dp', 'fsdp'))
- grad_expert_gate: float32 [16, 1024, 512], P('dp', 'fsdp')
- grad_expert_up: float32 [16, 1024, 512], P('dp', 'fsdp')
- grad_expert_down: float32 [16, 512, 1024], P('dp', 'fsdp')
Inputs may be any that keep to these rules, and one draw needn't show every extreme that they name: Within each block of 128 rows doc_id starts at 0 and never falls; live rows come first and carry ids below 128; the rows after them carry 128 (padding). Every block has 64 or more live rows and some block has no padding. `expert_ids`: each row names 8 different experts.
All inputs are finite; a program needn't handle non-finite values.
Results may differ from a plain program's by a relative error of at most 0.015.
The roundings to bfloat16 on the way count: a program that leaves them out, or rounds other values in their place, can miss the bound.
Values may be sent and summed in bfloat16 or wider, within the bound.
A program may use at most 128 MiB of HBM per device.

v0:
```python
import jax
import jax.numpy as jnp
from jax import lax
from jax.sharding import PartitionSpec as P

HEADS = 16
KV_HEADS = 8
HEAD_DIM = 64
TOP = 8
CAP = 24
norm_eps = 1e-05


def positions_mask(doc_block):
    row_count = doc_block.shape[0]
    row_index = jnp.arange(row_count)
    same_doc = doc_block[:, None] == doc_block[None, :]
    earlier = row_index[None, :] < row_index[:, None]
    position = jnp.sum((same_doc & earlier).astype(jnp.float32), axis=1)
    allowed = same_doc & (row_index[None, :] <= row_index[:, None])
    live_rows = (doc_block < row_count).astype(jnp.float32)
    return (position, allowed, live_rows)


def rope_tables(position):
    half_dim = HEAD_DIM // 2
    freqs = jnp.exp(-jnp.log(10000.0) * (2.0 * jnp.arange(half_dim, dtype=jnp.float32) / HEAD_DIM))
    angle = position[:, None] * freqs[None, :]
    return (jnp.cos(angle), jnp.sin(angle))


def rotate(values, cosine, sinusoid):
    half_dim = values.shape[-1] // 2
    first_half, second_half = (values[..., :half_dim], values[..., half_dim:])
    return jnp.concatenate(
        [
            first_half * cosine - second_half * sinusoid,
            second_half * cosine + first_half * sinusoid,
        ],
        axis=-1,
    )


def unrotate(values, cosine, sinusoid):
    half_dim = values.shape[-1] // 2
    first_half, second_half = (values[..., :half_dim], values[..., half_dim:])
    return jnp.concatenate(
        [
            first_half * cosine + second_half * sinusoid,
            second_half * cosine - first_half * sinusoid,
        ],
        axis=-1,
    )


def norm_forward(values, gain):
    scale_row = lax.rsqrt(jnp.mean(values * values, axis=-1, keepdims=True) + norm_eps)
    normed = values * scale_row
    return (normed, scale_row, (normed * gain).astype(jnp.bfloat16))


def norm_backward(upstream, normed, scale_row, gain):
    scaled = upstream * gain
    inner = jnp.mean(scaled * normed, axis=-1, keepdims=True)
    return (scale_row * (scaled - normed * inner), jnp.sum(upstream * normed, axis=0))


def probabilities(query_b, key_b, allowed, log_total):
    scores = jnp.einsum(
        "ikgd,jkd->kgij", query_b, key_b, preferred_element_type=jnp.float32
    ) * HEAD_DIM ** (-0.5)
    raised = jnp.where(allowed[None, None], jnp.exp(scores), 0.0)
    if log_total is None:
        log_total = jnp.log(jnp.sum(raised, axis=-1, keepdims=True))
    return (jnp.where(allowed[None, None], jnp.exp(scores - log_total), 0.0), log_total)


def routing(expert_block, live_rows, logits):
    experts = logits.shape[1]
    row_count = expert_block.shape[0]
    chosen = jnp.sum(
        (expert_block[:, :, None] == jnp.arange(experts)[None, None, :]).astype(jnp.float32), axis=1
    )
    raised = jnp.where(chosen > 0, jnp.exp(logits), 0.0)
    gates = raised / jnp.sum(raised, axis=1, keepdims=True)
    member = chosen * live_rows[:, None]
    lower = (jnp.arange(row_count)[None, :] < jnp.arange(row_count)[:, None]).astype(jnp.float32)
    rank = jnp.dot(lower, member, precision=lax.Precision.HIGHEST)
    kept = member * (rank < CAP).astype(jnp.float32)
    slot_match = (rank.T[:, None, :] == jnp.arange(CAP, dtype=jnp.float32)[None, :, None]).astype(
        jnp.float32
    )
    dispatch = kept.T[:, None, :] * slot_match
    return (gates, dispatch, kept, rank)


def expert_forward(rows_in, w_gate, w_up, w_down):
    gate_pre = jnp.dot(rows_in, w_gate, preferred_element_type=jnp.float32)
    up_pre = jnp.dot(rows_in, w_up, preferred_element_type=jnp.float32)
    act_rows = (jax.nn.silu(gate_pre) * up_pre).astype(jnp.bfloat16)
    out_rows = jnp.dot(act_rows, w_down, preferred_element_type=jnp.float32).astype(jnp.bfloat16)
    return (gate_pre, up_pre, act_rows, out_rows)


def expert_backward(rows_in, gate_pre, up_pre, act_rows, grad_rows, w_gate, w_up, w_down):
    grad_act = jnp.dot(grad_rows, w_down.T, preferred_element_type=jnp.float32)
    sigmoid_gate = jax.nn.sigmoid(gate_pre)
    grad_up_pre = (grad_act * gate_pre * sigmoid_gate).astype(jnp.bfloat16)
    grad_gate_pre = (
        grad_act * up_pre * sigmoid_gate * (1.0 + gate_pre * (1.0 - sigmoid_gate))
    ).astype(jnp.bfloat16)
    grad_down_w = jnp.dot(act_rows.T, grad_rows, preferred_element_type=jnp.float32)
    grad_gate_w = jnp.dot(rows_in.T, grad_gate_pre, preferred_element_type=jnp.float32)
    grad_up_w = jnp.dot(rows_in.T, grad_up_pre, preferred_element_type=jnp.float32)
    grad_rows_in = jnp.dot(grad_gate_pre, w_gate.T, preferred_element_type=jnp.float32)
    grad_rows_in = (
        grad_rows_in + jnp.dot(grad_up_pre, w_up.T, preferred_element_type=jnp.float32)
    ).astype(jnp.bfloat16)
    return (grad_rows_in, grad_gate_w, grad_up_w, grad_down_w)


def shards(
    hidden_in,
    doc_id,
    expert_ids,
    out_grad,
    attn_gain,
    query_weight,
    key_weight,
    value_weight,
    output_weight,
    ffn_gain,
    router_weight,
    expert_gate,
    expert_up,
    expert_down,
):
    rows = hidden_in.shape[0]
    groups = HEADS // KV_HEADS
    scale = HEAD_DIM ** (-0.5)
    dense_full = (
        lax.all_gather(attn_gain, ("dp", "fsdp"), axis=0, tiled=True),
        lax.all_gather(query_weight, ("dp", "fsdp"), axis=0, tiled=True),
        lax.all_gather(key_weight, ("dp", "fsdp"), axis=0, tiled=True),
        lax.all_gather(value_weight, ("dp", "fsdp"), axis=0, tiled=True),
        lax.all_gather(output_weight, ("dp", "fsdp"), axis=0, tiled=True),
        lax.all_gather(ffn_gain, ("dp", "fsdp"), axis=0, tiled=True),
        lax.all_gather(router_weight, ("dp", "fsdp"), axis=0, tiled=True),
    )
    expert_full = (
        lax.all_gather(expert_gate, "fsdp", axis=1, tiled=True),
        lax.all_gather(expert_up, "fsdp", axis=1, tiled=True),
        lax.all_gather(expert_down, "fsdp", axis=1, tiled=True),
    )
    gain_one, w_query, w_key, w_value, w_output, gain_two, w_router = dense_full
    w_gate, w_up, w_down = (expert_full[0][0], expert_full[1][0], expert_full[2][0])
    position, allowed, live_rows = positions_mask(doc_id)
    cosine, sinusoid = rope_tables(position)
    cos_query, sin_query = (cosine[:, None, None, :], sinusoid[:, None, None, :])
    cos_key, sin_key = (cosine[:, None, :], sinusoid[:, None, :])
    resid_in = hidden_in.astype(jnp.float32)
    normed_one, scale_one, normed_in = norm_forward(resid_in, gain_one.astype(jnp.float32))
    query_raw = jnp.dot(normed_in, w_query, preferred_element_type=jnp.float32).reshape(
        rows, KV_HEADS, groups, HEAD_DIM
    )
    key_raw = jnp.dot(normed_in, w_key, preferred_element_type=jnp.float32).reshape(
        rows, KV_HEADS, HEAD_DIM
    )
    query_b = rotate(query_raw, cos_query, sin_query).astype(jnp.bfloat16)
    key_b = rotate(key_raw, cos_key, sin_key).astype(jnp.bfloat16)
    value_b = (
        jnp.dot(normed_in, w_value, preferred_element_type=jnp.float32)
        .reshape(rows, KV_HEADS, HEAD_DIM)
        .astype(jnp.bfloat16)
    )
    probs, log_total = probabilities(query_b, key_b, allowed, None)
    probs_b = probs.astype(jnp.bfloat16)
    mixed = jnp.einsum("kgij,jkd->ikgd", probs_b, value_b, preferred_element_type=jnp.float32)
    mixed_b = (
        (mixed * live_rows[:, None, None, None])
        .reshape(rows, HEADS * HEAD_DIM)
        .astype(jnp.bfloat16)
    )
    resid_mid = resid_in + jnp.dot(mixed_b, w_output, preferred_element_type=jnp.float32)
    normed_two, scale_two, routed_in = norm_forward(resid_mid, gain_two.astype(jnp.float32))
    logits = jnp.dot(routed_in, w_router, preferred_element_type=jnp.float32)
    gates, dispatch, kept, rank = routing(expert_ids, live_rows, logits)
    dispatch_b = dispatch.astype(jnp.bfloat16)
    send_rows = jnp.einsum(
        "ecr,rd->ecd", dispatch_b, routed_in, preferred_element_type=jnp.float32
    ).astype(jnp.bfloat16)
    recv_rows = lax.all_to_all(send_rows, "dp", split_axis=0, concat_axis=0, tiled=True)
    flat_in = recv_rows.reshape(-1, recv_rows.shape[2])
    gate_pre, up_pre, act_rows, out_rows = expert_forward(flat_in, w_gate, w_up, w_down)
    back_rows = lax.all_to_all(
        out_rows.reshape(recv_rows.shape), "dp", split_axis=0, concat_axis=0, tiled=True
    )
    experts = back_rows.shape[0]
    capacity = back_rows.shape[1]
    width = back_rows.shape[2]
    chosen_slot = (expert_ids[:, :, None] == jnp.arange(experts)[None, None, :]).astype(jnp.float32)
    gate_pick = jnp.sum(chosen_slot * (gates * kept)[:, None, :], axis=2)
    rank_pick = jnp.sum(chosen_slot * rank[:, None, :], axis=2)
    slot_index = expert_ids * capacity + jnp.minimum(rank_pick, capacity - 1.0).astype(jnp.int32)
    back_flat = back_rows.reshape(experts * capacity, width)
    picked_rows = jnp.take(back_flat, slot_index.reshape(-1), axis=0).reshape(rows, TOP, width)
    expert_sum = jnp.sum(gate_pick[:, :, None] * picked_rows.astype(jnp.float32), axis=1)
    layer_out = (resid_mid + expert_sum).astype(jnp.bfloat16)
    dense_full = (
        lax.all_gather(attn_gain, ("dp", "fsdp"), axis=0, tiled=True),
        lax.all_gather(query_weight, ("dp", "fsdp"), axis=0, tiled=True),
        lax.all_gather(key_weight, ("dp", "fsdp"), axis=0, tiled=True),
        lax.all_gather(value_weight, ("dp", "fsdp"), axis=0, tiled=True),
        lax.all_gather(output_weight, ("dp", "fsdp"), axis=0, tiled=True),
        lax.all_gather(ffn_gain, ("dp", "fsdp"), axis=0, tiled=True),
        lax.all_gather(router_weight, ("dp", "fsdp"), axis=0, tiled=True),
    )
    expert_full = (
        lax.all_gather(expert_gate, "fsdp", axis=1, tiled=True),
        lax.all_gather(expert_up, "fsdp", axis=1, tiled=True),
        lax.all_gather(expert_down, "fsdp", axis=1, tiled=True),
    )
    gain_one, w_query, w_key, w_value, w_output, gain_two, w_router = dense_full
    w_gate, w_up, w_down = (expert_full[0][0], expert_full[1][0], expert_full[2][0])
    grad_out = out_grad.astype(jnp.float32)
    slot_gate = jnp.sum(dispatch * gates.T[:, None, :], axis=2)
    pulled_grad = jnp.einsum(
        "ecr,rd->ecd", dispatch_b, out_grad, preferred_element_type=jnp.float32
    )
    grad_send = (slot_gate[:, :, None] * pulled_grad).astype(jnp.bfloat16)
    slot_dot = jnp.sum(back_rows.astype(jnp.float32) * pulled_grad, axis=2)
    grad_gates = jnp.sum(dispatch * slot_dot[:, :, None], axis=1).T
    grad_logits = gates * (grad_gates - jnp.sum(gates * grad_gates, axis=1, keepdims=True))
    grad_logits_b = grad_logits.astype(jnp.bfloat16)
    grad_recv = lax.all_to_all(grad_send, "dp", split_axis=0, concat_axis=0, tiled=True)
    grad_rows_in, grad_gate_w, grad_up_w, grad_down_w = expert_backward(
        flat_in, gate_pre, up_pre, act_rows, grad_recv.reshape(flat_in.shape), w_gate, w_up, w_down
    )
    grad_back = lax.all_to_all(
        grad_rows_in.reshape(recv_rows.shape), "dp", split_axis=0, concat_axis=0, tiled=True
    )
    grad_routed = jnp.einsum(
        "ecr,ecd->rd", dispatch_b, grad_back, preferred_element_type=jnp.float32
    )
    grad_routed = grad_routed + jnp.dot(
        grad_logits_b, w_router.T, preferred_element_type=jnp.float32
    )
    grad_w_router = jnp.dot(routed_in.T, grad_logits_b, preferred_element_type=jnp.float32)
    grad_norm_two, grad_gain_two = norm_backward(
        grad_routed, normed_two, scale_two, gain_two.astype(jnp.float32)
    )
    grad_mid = grad_out + grad_norm_two
    grad_mid_b = grad_mid.astype(jnp.bfloat16)
    grad_w_output = jnp.dot(mixed_b.T, grad_mid_b, preferred_element_type=jnp.float32)
    grad_mixed = jnp.dot(grad_mid_b, w_output.T, preferred_element_type=jnp.float32).reshape(
        rows, KV_HEADS, groups, HEAD_DIM
    )
    grad_mixed = (grad_mixed * live_rows[:, None, None, None]).astype(jnp.bfloat16)
    probs_again, unused_total = probabilities(query_b, key_b, allowed, log_total)
    grad_probs = jnp.einsum(
        "ikgd,jkd->kgij", grad_mixed, value_b, preferred_element_type=jnp.float32
    )
    delta = jnp.sum(probs_again * grad_probs, axis=-1, keepdims=True)
    grad_scores = (probs_again * (grad_probs - delta) * scale).astype(jnp.bfloat16)
    grad_query_raw = jnp.einsum(
        "kgij,jkd->ikgd", grad_scores, key_b, preferred_element_type=jnp.float32
    )
    grad_key_raw = jnp.einsum(
        "kgij,ikgd->jkd", grad_scores, query_b, preferred_element_type=jnp.float32
    )
    grad_value_raw = jnp.einsum(
        "kgij,ikgd->jkd",
        probs_again.astype(jnp.bfloat16),
        grad_mixed,
        preferred_element_type=jnp.float32,
    )
    grad_query_b = (
        unrotate(grad_query_raw, cos_query, sin_query)
        .reshape(rows, HEADS * HEAD_DIM)
        .astype(jnp.bfloat16)
    )
    grad_key_b = (
        unrotate(grad_key_raw, cos_key, sin_key)
        .reshape(rows, KV_HEADS * HEAD_DIM)
        .astype(jnp.bfloat16)
    )
    grad_value_b = grad_value_raw.reshape(rows, KV_HEADS * HEAD_DIM).astype(jnp.bfloat16)
    grad_w_query = jnp.dot(normed_in.T, grad_query_b, preferred_element_type=jnp.float32)
    grad_w_key = jnp.dot(normed_in.T, grad_key_b, preferred_element_type=jnp.float32)
    grad_w_value = jnp.dot(normed_in.T, grad_value_b, preferred_element_type=jnp.float32)
    grad_normed = jnp.dot(grad_query_b, w_query.T, preferred_element_type=jnp.float32)
    grad_normed = grad_normed + jnp.dot(grad_key_b, w_key.T, preferred_element_type=jnp.float32)
    grad_normed = grad_normed + jnp.dot(grad_value_b, w_value.T, preferred_element_type=jnp.float32)
    grad_norm_one, grad_gain_one = norm_backward(
        grad_normed, normed_one, scale_one, gain_one.astype(jnp.float32)
    )
    grad_input = (grad_mid + grad_norm_one).astype(jnp.bfloat16)
    dense_grads = (
        lax.psum_scatter(grad_gain_one, ("dp", "fsdp"), scatter_dimension=0, tiled=True),
        lax.psum_scatter(grad_w_query, ("dp", "fsdp"), scatter_dimension=0, tiled=True),
        lax.psum_scatter(grad_w_key, ("dp", "fsdp"), scatter_dimension=0, tiled=True),
        lax.psum_scatter(grad_w_value, ("dp", "fsdp"), scatter_dimension=0, tiled=True),
        lax.psum_scatter(grad_w_output, ("dp", "fsdp"), scatter_dimension=0, tiled=True),
        lax.psum_scatter(grad_gain_two, ("dp", "fsdp"), scatter_dimension=0, tiled=True),
        lax.psum_scatter(grad_w_router, ("dp", "fsdp"), scatter_dimension=0, tiled=True),
    )
    expert_grads = (
        lax.psum_scatter(
            grad_gate_w[None].astype(jnp.bfloat16), "fsdp", scatter_dimension=1, tiled=True
        ).astype(jnp.float32),
        lax.psum_scatter(
            grad_up_w[None].astype(jnp.bfloat16), "fsdp", scatter_dimension=1, tiled=True
        ).astype(jnp.float32),
        lax.psum_scatter(
            grad_down_w[None].astype(jnp.bfloat16), "fsdp", scatter_dimension=1, tiled=True
        ).astype(jnp.float32),
    )
    return (
        layer_out,
        grad_input,
        dense_grads[0],
        dense_grads[1],
        dense_grads[2],
        dense_grads[3],
        dense_grads[4],
        dense_grads[5],
        dense_grads[6],
        expert_grads[0],
        expert_grads[1],
        expert_grads[2],
    )


def solution(mesh):
    in_specs = (
        P(("dp", "fsdp"), None),
        P(("dp", "fsdp")),
        P(("dp", "fsdp"), None),
        P(("dp", "fsdp"), None),
        P(("dp", "fsdp")),
        P(("dp", "fsdp"), None),
        P(("dp", "fsdp"), None),
        P(("dp", "fsdp"), None),
        P(("dp", "fsdp"), None),
        P(("dp", "fsdp")),
        P(("dp", "fsdp"), None),
        P("dp", "fsdp", None),
        P("dp", "fsdp", None),
        P("dp", "fsdp", None),
    )
    out_specs = (
        P(("dp", "fsdp"), None),
        P(("dp", "fsdp"), None),
        P(("dp", "fsdp")),
        P(("dp", "fsdp"), None),
        P(("dp", "fsdp"), None),
        P(("dp", "fsdp"), None),
        P(("dp", "fsdp"), None),
        P(("dp", "fsdp")),
        P(("dp", "fsdp"), None),
        P("dp", "fsdp", None),
        P("dp", "fsdp", None),
        P("dp", "fsdp", None),
    )
    return jax.shard_map(shards, mesh=mesh, in_specs=in_specs, out_specs=out_specs, check_vma=False)
```

profile of v0, /device:TPU:0, one launch (start us, length us, event | category | flops | bytes accessed | tf_op | source)
XLA Modules:
  0.0 1174.7 jit_solution(4902561280423588323)
XLA Ops:
  15.2 41.9 %all-reduce.5 = (bf16[1024]{0:T(1024)(128)(2,1)S(1)}, bf16[1024]{0:T(1024)(128)(2,1)S(1)}) all-reduce(bf16[1024]{0:T(1024)(128)(2,1)S(1)} %dynamic-update-slice, bf16[1024]{0:T(1024)(128)(2,1)S(1)} %dynamic-update-slice.1), channel_id=1, replica_groups=mesh['dp'=16,'fsdp'=2] {'dp','fsdp'}, use_global_device_ids=true, to_apply=%add | all-reduce | flops 2048 | bytes 8192
  59.3 8.2 all-gather.9.cloned.1.call-done
  67.5 1.7 convolution_convert_fusion.5
  69.3 54.0 %all-gather.11.cloned.1.call-done = bf16[1024,512]{1,0:T(8,128)(2,1)} async-done(((bf16[32,512]{1,0:T(8,128)(2,1)}), bf16[1024,512]{1,0:T(8,128)(2,1)}) %all-gather.11.cloned.1.call-update) | async-done | bytes 1048592 | tf_op jit(solution)/shard_map/all_gather | solution.py:144
  123.2 1.8 fusion.99
  125.1 56.5 %all-gather.13.cloned.1.call-done = bf16[1024,1024]{1,0:T(8,128)(2,1)} async-done(((bf16[32,1024]{1,0:T(8,128)(2,1)}), bf16[1024,1024]{1,0:T(8,128)(2,1)}) %all-gather.13.cloned.1.call-update) | async-done | bytes 2097168 | tf_op jit(solution)/shard_map/all_gather | solution.py:143
  181.6 2.6 fusion.97
  185.5 54.2 %all-gather.15.cloned.1.call-done = bf16[1024,1024]{1,0:T(8,128)(2,1)} async-done(((bf16[32,1024]{1,0:T(8,128)(2,1)}), bf16[1024,1024]{1,0:T(8,128)(2,1)}) %all-gather.15.cloned.1.call-update) | async-done | bytes 2097168 | tf_op jit(solution)/shard_map/all_gather | solution.py:146
  239.7 2.1 multiply_reduce_fusion.5
  244.0 4.5 all-to-all-start
  249.2 12.0 %all-gather.17.cloned.1.call-done = bf16[1,1024,512]{2,1,0:T(8,128)(2,1)} async-done(((bf16[1,512,512]{2,1,0:T(8,128)(2,1)}), bf16[1,1024,512]{2,1,0:T(8,128)(2,1)}) %all-gather.17.cloned.1.call-update) | async-done | bytes 1048592 | tf_op jit(solution)/shard_map/all_gather | solution.py:151
  261.2 5.9 all-to-all-done
  267.1 1.8 fusion.25
  268.9 15.0 %all-gather.19.cloned.1.call-done = bf16[1,1024,512]{2,1,0:T(8,128)(2,1)} async-done(((bf16[1,512,512]{2,1,0:T(8,128)(2,1)}), bf16[1,1024,512]{2,1,0:T(8,128)(2,1)}) %all-gather.19.cloned.1.call-update) | async-done | bytes 1048592 | tf_op jit(solution)/shard_map/all_gather | solution.py:152
  284.0 2.7 multiply_convert_fusion.3
  286.6 20.2 %all-gather.21.cloned.1.call-done = bf16[1,512,1024]{2,1,0:T(8,128)(2,1)} async-done(((bf16[1,256,1024]{2,1,0:T(8,128)(2,1)}), bf16[1,512,1024]{2,1,0:T(8,128)(2,1)}) %all-gather.21.cloned.1.call-update) | async-done | bytes 1048592 | tf_op jit(solution)/shard_map/all_gather | solution.py:153
  306.8 2.8 convolution_convert_fusion.3
  309.6 5.6 all-to-all-start.1
  315.2 76.2 %all-gather = bf16[32,32,16]{1,2,0:T(8,128)(2,1)S(1)} all-gather(bf16[1,32,16]{1,2,0:T(8,128)(2,1)S(1)} %bitcast.165), channel_id=1, replica_groups=mesh['dp'=16,'fsdp'=2] {'dp','fsdp'}, dimensions={0}, use_global_device_ids=true | all-gather | bytes 33792 | tf_op jit(solution)/shard_map/all_gather | solution.py:148
  393.6 3.6 all-to-all-start.2
  399.0 16.8 %all-to-all-done.2 = bf16[16,24,1024]{2,1,0:T(8,128)(2,1)S(1)} async-done(((bf16[16,24,1024]{2,1,0:T(8,128)(2,1)}), bf16[16,24,1024]{2,1,0:T(8,128)(2,1)S(1)}, u32[]{:S(2)}, u32[]{:S(2)}) %all-to-all-start.2) | async-done | bytes 786464 | tf_op jit(solution)/shard_map/all_to_all | solution.py:235
  415.8 2.8 multiply_convert_fusion.1
  419.4 1.7 fusion.2
  421.2 1.7 fusion.3
  423.0 1.7 fusion.23
  424.7 1.5 add_convert_fusion
  426.2 5.7 all-to-all-start.3
  433.9 4.1 gather_fusion
  438.0 2.3 multiply_reduce_fusion
  440.3 1.7 fusion.4
  442.1 8.6 all-to-all-done.3
  455.4 2.1 convolution_bitcast_fusion.4
  457.6 1.9 fusion.93
  459.6 2.1 fusion.15
  461.6 1.9 fusion.91
  463.6 2.1 convolution_bitcast_fusion.1
  465.8 2.8 fusion.95
  469.6 2.7 fusion.56
  472.3 65.3 %reduce-scatter.25.cloned.1.call-done = f32[32,16]{1,0:T(8,128)} async-done(((f32[1024,16]{1,0:T(8,128)}), f32[32,16]{1,0:T(8,128)}) %reduce-scatter.25.cloned.1.call-update) | async-done | bytes 2064
  541.4 38.1 %all-reduce.4 = (f32[1024]{0:T(1024)S(1)}, f32[1024]{0:T(1024)S(1)}) all-reduce(f32[1024]{0:T(1024)S(1)} %get-tuple-element.14, f32[1024]{0:T(1024)S(1)} %copy-done.49), channel_id=2, replica_groups=mesh['dp'=16,'fsdp'=2] {'dp','fsdp'}, use_global_device_ids=true, to_apply=%region_17.18.clone | all-reduce | flops 2048 | bytes 16384
  581.6 2.1 convert_element_type.188
  583.7 2.1 convert_element_type.191
  585.9 17.1 %reduce-scatter.23.cloned.1.call-done = bf16[1,256,1024]{2,1,0:T(8,128)(2,1)} async-done(((bf16[1,512,1024]{2,1,0:T(8,128)(2,1)}), bf16[1,256,1024]{2,1,0:T(8,128)(2,1)}) %reduce-scatter.23.cloned.1.call-update) | async-done | bytes 524304 | tf_op jit(solution)/shard_map/reduce_scatter | solution.py:314
  602.9 2.1 convert_element_type.194
  605.0 139.8 %reduce-scatter.13.cloned.1.call-done = f32[32,512]{1,0:T(8,128)} async-done(((f32[1024,512]{1,0:T(8,128)}), f32[32,512]{1,0:T(8,128)}) %reduce-scatter.13.cloned.1.call-update) | async-done | bytes 65552 | tf_op jit(solution)/shard_map/reduce_scatter | solution.py:301
  744.9 137.4 %reduce-scatter.15.cloned.1.call-done = f32[32,512]{1,0:T(8,128)} async-done(((f32[1024,512]{1,0:T(8,128)}), f32[32,512]{1,0:T(8,128)}) %reduce-scatter.15.cloned.1.call-update) | async-done | bytes 65552 | tf_op jit(solution)/shard_map/reduce_scatter | solution.py:302
  882.3 142.9 %reduce-scatter.11.cloned.1.call-done = f32[32,1024]{1,0:T(8,128)} async-done(((f32[1024,1024]{1,0:T(8,128)}), f32[32,1024]{1,0:T(8,128)}) %reduce-scatter.11.cloned.1.call-update) | async-done | bytes 131088 | tf_op jit(solution)/shard_map/reduce_scatter | solution.py:300
  1025.2 143.0 %reduce-scatter.17.cloned.1.call-done = f32[32,1024]{1,0:T(8,128)} async-done(((f32[1024,1024]{1,0:T(8,128)}), f32[32,1024]{1,0:T(8,128)}) %reduce-scatter.17.cloned.1.call-update) | async-done | bytes 131088 | tf_op jit(solution)/shard_map/reduce_scatter | solution.py:303
  (207 shorter events, 32.5 us)
Async XLA Ops:
  7.2 116.1 %copy-start = (bf16[128,1024]{1,0:T(8,128)(2,1)S(1)}, bf16[128,1024]{1,0:T(8,128)(2,1)}, u32[]{:S(2)}) copy-start(bf16[128,1024]{1,0:T(8,128)(2,1)} %param.14) | copy-start | bytes 786436
  7.2 60.3 %all-gather.9.cloned.1.call-start = ((), (), s32[]{:S(2)}) async-start(), calls=%async_computation.12 | async-start | bytes 1081344 | tf_op jit(solution)/shard_map/all_gather | solution.py:145
  7.9 115.3 %all-gather.11.cloned.1.call-start = ((), (), s32[]{:S(2)}) async-start(), calls=%async_computation.13 | async-start | bytes 1081344 | tf_op jit(solution)/shard_map/all_gather | solution.py:144
  8.7 172.9 %all-gather.13.cloned.1.call-start = ((), (), s32[]{:S(2)}) async-start(), calls=%async_computation.14 | async-start | bytes 2162688 | tf_op jit(solution)/shard_map/all_gather | solution.py:143
  9.4 230.3 %all-gather.15.cloned.1.call-start = ((), (), s32[]{:S(2)}) async-start(), calls=%async_computation.15 | async-start | bytes 2162688 | tf_op jit(solution)/shard_map/all_gather | solution.py:146
  10.0 251.3 %all-gather.17.cloned.1.call-start = ((), (), s32[]{:S(2)}) async-start(), calls=%async_computation.16 | async-start | bytes 1572864 | tf_op jit(solution)/shard_map/all_gather | solution.py:151
  10.6 273.4 %all-gather.19.cloned.1.call-start = ((), (), s32[]{:S(2)}) async-start(), calls=%async_computation.17 | async-start | bytes 1572864 | tf_op jit(solution)/shard_map/all_gather | solution.py:152
  11.8 385.4 %copy-start.55 = (f32[128]{0:T(128)}, f32[128]{0:T(128)S(1)}, u32[]{:S(2)}) copy-start(f32[128]{0:T(128)S(1)} %compare_convert_fusion) | copy-start | bytes 1540
  13.5 171.5 %copy-start.50 = (pred[128,128]{0,1:T(8,128)(4,1)}, pred[128,128]{0,1:T(8,128)(4,1)S(1)}, u32[]{:S(2)}) copy-start(pred[128,128]{0,1:T(8,128)(4,1)S(1)} %compare_and_fusion.1) | copy-start | bytes 49156
  57.1 127.1 %copy-start.29 = (f32[1024]{0:T(1024)}, f32[1024]{0:T(1024)S(1)}, u32[]{:S(2)}) copy-start(f32[1024]{0:T(1024)S(1)} %convert_element_type.150) | copy-start | bytes 12292
  58.2 126.0 %copy-start.47 = (f32[128]{0:T(128)}, f32[128]{0:T(128)S(1)}, u32[]{:S(2)}) copy-start(f32[128]{0:T(128)S(1)} %add_rsqrt_fusion.1) | copy-start | bytes 1540
  58.2 183.6 %copy-start.41 = (f32[1024]{0:T(1024)}, f32[1024]{0:T(1024)S(1)}, u32[]{:S(2)}) copy-start(f32[1024]{0:T(1024)S(1)} %convert_element_type.161) | copy-start | bytes 12292
  59.1 125.1 %copy-start.25 = (f32[128,32]{0,1:T(8,128)}, f32[128,32]{0,1:T(8,128)S(1)}, u32[]{:S(2)}) copy-start(f32[128,32]{0,1:T(8,128)S(1)} %get-tuple-element.41) | copy-start | bytes 49156
  59.2 333.1 %copy-start.39 = (f32[16,128]{1,0:T(8,128)}, f32[16,128]{1,0:T(8,128)S(1)}, u32[]{:S(2)}) copy-start(f32[16,128]{1,0:T(8,128)S(1)} %get-tuple-element.42) | copy-start | bytes 24580
  59.2 338.0 %copy-start.33 = (f32[128,16]{0,1:T(8,128)}, f32[128,16]{0,1:T(8,128)S(1)}, u32[]{:S(2)}) copy-start(f32[128,16]{0,1:T(8,128)S(1)} %get-tuple-element.43) | copy-start | bytes 24580
  69.3 115.7 %copy-start.19 = (bf16[128,512]{0,1:T(8,128)(2,1)}, bf16[128,512]{0,1:T(8,128)(2,1)S(1)}, u32[]{:S(2)}) copy-start(bf16[128,512]{0,1:T(8,128)(2,1)S(1)} %copy.69) | copy-start | bytes 393220
  125.1 59.5 %copy-start.35 = (bf16[128,8,32]{0,2,1:T(8,128)(2,1)}, bf16[128,8,32]{0,2,1:T(8,128)(2,1)S(1)}, u32[]{:S(2)}) copy-start(bf16[128,8,32]{0,2,1:T(8,128)(2,1)S(1)} %get-tuple-element.36) | copy-start | bytes 196612
  125.1 59.5 %copy-start.37 = (bf16[128,8,32]{0,2,1:T(8,128)(2,1)}, bf16[128,8,32]{0,2,1:T(8,128)(2,1)S(1)}, u32[]{:S(2)}) copy-start(bf16[128,8,32]{0,2,1:T(8,128)(2,1)S(1)} %get-tuple-element.37) | copy-start | bytes 196612
  185.0 56.9 %copy-start.13 = (f32[8,2,128,128]{2,3,1,0:T(8,128)}, f32[8,2,128,128]{2,3,1,0:T(8,128)S(1)}, u32[]{:S(2)}) copy-start(f32[8,2,128,128]{2,3,1,0:T(8,128)S(1)} %fusion.12) | copy-start | bytes 3145732
  185.5 58.5 %copy-start.16 = (bf16[8,64,2,128]{3,1,2,0:T(8,128)(2,1)}, bf16[8,64,2,128]{3,1,2,0:T(8,128)(2,1)S(1)}, u32[]{:S(2)}) copy-start(bf16[8,64,2,128]{3,1,2,0:T(8,128)(2,1)S(1)} %fusion.14) | copy-start | bytes 786436
  244.0 23.2 %all-to-all-start = ((bf16[16,24,1024]{2,1,0:T(8,128)(2,1)}), bf16[16,24,1024]{2,1,0:T(8,128)(2,1)S(1)}, u32[]{:S(2)}, u32[]{:S(2)}) async-start(bf16[16,24,1024]{2,1,0:T(8,128)(2,1)} %convolution_convert_fusion.4), calls=%async_computation | async-start | bytes 1572864 | tf_op jit(solution)/shard_map/all_to_all | solution.py:192
  248.5 58.3 %all-gather.21.cloned.1.call-start = ((), (), s32[]{:S(2)}) async-start(), calls=%async_computation.18 | async-start | bytes 1572864 | tf_op jit(solution)/shard_map/all_gather | solution.py:153
  268.9 17.7 %copy-start.18 = (f32[384,512]{1,0:T(8,128)}, f32[384,512]{1,0:T(8,128)S(1)}, u32[]{:S(2)}) copy-start(f32[384,512]{1,0:T(8,128)S(1)} %fusion.25) | copy-start | bytes 2359300
  286.6 28.6 %copy-start.27 = (bf16[384,512]{1,0:T(8,128)(2,1)}, bf16[384,512]{1,0:T(8,128)(2,1)S(1)}, u32[]{:S(2)}) copy-start(bf16[384,512]{1,0:T(8,128)(2,1)S(1)} %get-tuple-element.46) | copy-start | bytes 1179652
  286.6 28.6 %copy-start.54 = (bf16[32,16]{0,1:T(8,128)(2,1)S(1)}, bf16[32,16]{0,1:T(8,128)(2,1)}, u32[]{:S(2)}) copy-start(bf16[32,16]{0,1:T(8,128)(2,1)} %param.24) | copy-start | bytes 3076
  306.8 85.0 %copy-start.12 = (bf16[128,1024]{1,0:T(8,128)(2,1)S(1)}, bf16[128,1024]{1,0:T(8,128)(2,1)}, u32[]{:S(2)}) copy-start(bf16[128,1024]{1,0:T(8,128)(2,1)} %param.17) | copy-start | bytes 786436
  309.6 82.3 %all-to-all-start.1 = ((bf16[16,24,1024]{2,1,0:T(8,128)(2,1)}), bf16[16,24,1024]{2,1,0:T(8,128)(2,1)S(1)}, u32[]{:S(2)}, u32[]{:S(2)}) async-start(bf16[16,24,1024]{2,1,0:T(8,128)(2,1)} %bitcast.18), calls=%async_computation.1 | async-start | bytes 1572864 | tf_op jit(solution)/shard_map/all_to_all | solution.py:195
  393.6 22.3 %all-to-all-start.2 = ((bf16[16,24,1024]{2,1,0:T(8,128)(2,1)}), bf16[16,24,1024]{2,1,0:T(8,128)(2,1)S(1)}, u32[]{:S(2)}, u32[]{:S(2)}) async-start(bf16[16,24,1024]{2,1,0:T(8,128)(2,1)} %multiply_convert_fusion), calls=%async_computation.2 | async-start | bytes 1572864 | tf_op jit(solution)/shard_map/all_to_all | solution.py:235
  397.2 140.4 %reduce-scatter.25.cloned.1.call-start = ((), (), s32[]{:S(2)}) async-start(), calls=%async_computation.26 | async-start | bytes 540672
  397.9 17.9 %copy-start.43 = (bf16[128,16]{0,1:T(8,128)(2,1)}, bf16[128,16]{0,1:T(8,128)(2,1)S(1)}, u32[]{:S(2)}) copy-start(bf16[128,16]{0,1:T(8,128)(2,1)S(1)} %get-tuple-element.38) | copy-start | bytes 12292
  399.0 182.6 %reduce-scatter.19.cloned.1.call-start = ((), (), s32[]{:S(2)}) async-start(), calls=%async_computation.23 | async-start | bytes 1572864 | tf_op jit(solution)/shard_map/reduce_scatter | solution.py:308
  421.2 162.6 %reduce-scatter.21.cloned.1.call-start = ((), (), s32[]{:S(2)}) async-start(), calls=%async_computation.24 | async-start | bytes 1572864 | tf_op jit(solution)/shard_map/reduce_scatter | solution.py:311
  424.7 7.4 copy-start.14
  424.7 7.4 copy-start.51
  426.2 24.5 %all-to-all-start.3 = ((bf16[16,24,1024]{2,1,0:T(8,128)(2,1)}), bf16[16,24,1024]{2,1,0:T(8,128)(2,1)}, u32[]{:S(2)}, u32[]{:S(2)}) async-start(bf16[16,24,1024]{2,1,0:T(8,128)(2,1)} %bitcast.25), calls=%async_computation.3 | async-start | bytes 1572864 | tf_op jit(solution)/shard_map/all_to_all | solution.py:239
  432.0 170.9 %reduce-scatter.23.cloned.1.call-start = ((), (), s32[]{:S(2)}) async-start(), calls=%async_computation.25 | async-start | bytes 1572864 | tf_op jit(solution)/shard_map/reduce_scatter | solution.py:314
  440.3 10.4 copy-start.40
  440.3 11.9 %copy-start.4 = (f32[128,1024]{1,0:T(8,128)S(1)}, f32[128,1024]{1,0:T(8,128)}, u32[]{:S(2)}) copy-start(f32[128,1024]{1,0:T(8,128)} %copy-done.3) | copy-start | bytes 1572868
  440.3 11.9 %copy-start.32 = (bf16[1024,16]{0,1:T(8,128)(2,1)S(1)}, bf16[1024,16]{0,1:T(8,128)(2,1)}, u32[]{:S(2)}) copy-start(bf16[1024,16]{0,1:T(8,128)(2,1)} %copy-done.31) | copy-start | bytes 98308
  440.3 11.9 %copy-start.42 = (f32[1024]{0:T(1024)S(1)}, f32[1024]{0:T(1024)}, u32[]{:S(2)}) copy-start(f32[1024]{0:T(1024)} %copy-done.41) | copy-start | bytes 12292
  440.3 11.9 %copy-start.44 = (bf16[128,16]{0,1:T(8,128)(2,1)S(1)}, bf16[128,16]{0,1:T(8,128)(2,1)}, u32[]{:S(2)}) copy-start(bf16[128,16]{0,1:T(8,128)(2,1)} %copy-done.43) | copy-start | bytes 12292
  440.3 11.9 %copy-start.53 = (f32[128]{0:T(128)S(1)}, f32[128]{0:T(128)}, u32[]{:S(2)}) copy-start(f32[128]{0:T(128)} %copy-done.52) | copy-start | bytes 1540
  442.0 11.1 copy-start.10
  442.1 302.8 %reduce-scatter.13.cloned.1.call-start = ((), (), s32[]{:S(2)}) async-start(), calls=%async_computation.20 | async-start | bytes 2162688 | tf_op jit(solution)/shard_map/reduce_scatter | solution.py:301
  459.5 422.8 %reduce-scatter.15.cloned.1.call-start = ((), (), s32[]{:S(2)}) async-start(), calls=%async_computation.21 | async-start | bytes 2162688 | tf_op jit(solution)/shard_map/reduce_scatter | solution.py:302
  463.5 561.6 %reduce-scatter.11.cloned.1.call-start = ((), (), s32[]{:S(2)}) async-start(), calls=%async_computation.19 | async-start | bytes 4325376 | tf_op jit(solution)/shard_map/reduce_scatter | solution.py:300
  468.6 699.5 %reduce-scatter.17.cloned.1.call-start = ((), (), s32[]{:S(2)}) async-start(), calls=%async_computation.22 | async-start | bytes 4325376 | tf_op jit(solution)/shard_map/reduce_scatter | solution.py:303
  472.3 66.7 %copy-start.1 = (bf16[1024,1024]{1,0:T(8,128)(2,1)S(1)}, bf16[1024,1024]{1,0:T(8,128)(2,1)}, u32[]{:S(2)}) copy-start(bf16[1024,1024]{1,0:T(8,128)(2,1)} %all-gather.13.cloned.1.call-done) | copy-start | bytes 6291460
  (28 other events, 62.5 us)
Sparse Core Ops, SparseCore 0:
  10.9 56.5 all-gather.8
  70.4 52.8 all-gather.10
  126.2 55.3 all-gather.12
  184.4 55.1 all-gather.14
  241.1 20.1 all-gather.16
  262.6 21.2 all-gather.18
  285.5 21.2 all-gather.20
  400.3 137.3 reduce-scatter.24
  540.4 17.0 reduce-scatter.18
  559.6 20.5 reduce-scatter.20
  582.4 20.4 reduce-scatter.22
  605.6 139.2 reduce-scatter.12
  747.7 134.5 reduce-scatter.14
  885.0 140.1 reduce-scatter.10
  1027.9 140.2 reduce-scatter.16
where the time goes:
time: 1180 us; the launch traced here: 1170 us
  waiting for transfers between devices  901 us (76%)
  blocking collectives  156 us (13%)
  matrix products  51.4 us (4%)
  starting transfers between devices  20 us (2%)
  other arithmetic  18.5 us (2%)
  between operations  14.8 us (1%)
  local copies, waits for them, and re-layouts  12.5 us (1%)
    reduce_scatter x1, waiting for transfers between devices, shards(): lax.psum_scatter(grad_w_output, ('dp', 'fsdp'), scatter_dimension=0, tile...  143 us
    reduce_scatter x1, waiting for transfers between devices, shards(): lax.psum_scatter(grad_w_query, ('dp', 'fsdp'), scatter_dimension=0, tiled...  143 us
    reduce_scatter x1, waiting for transfers between devices, shards(): lax.psum_scatter(grad_w_key, ('dp', 'fsdp'), scatter_dimension=0, tiled=T...  140 us
    reduce_scatter x1, waiting for transfers between devices, shards(): lax.psum_scatter(grad_w_value, ('dp', 'fsdp'), scatter_dimension=0, tiled...  137 us
    unnamed x2, blocking collectives  80 us
    all_gather x1, blocking collectives, shards(): lax.all_gather(router_weight, ('dp', 'fsdp'), axis=0, tiled=True)  76.2 us
    unnamed x16, waiting for transfers between devices  69.8 us
    all_gather x1, waiting for transfers between devices, shards(): lax.all_gather(query_weight, ('dp', 'fsdp'), axis=0, tiled=True)  56.5 us
  transfers between devices with their start and end apart: 19, of which 16 were waited for; matrix products, arithmetic and copies ran while one was open for 6% of the time, Pallas kernels for 0%

commit v1 on v0

--- a/solution.py
+++ b/solution.py
@@ -145,7 +145,12 @@
         lax.all_gather(value_weight, ("dp", "fsdp"), axis=0, tiled=True),
         lax.all_gather(output_weight, ("dp", "fsdp"), axis=0, tiled=True),
         lax.all_gather(ffn_gain, ("dp", "fsdp"), axis=0, tiled=True),
-        lax.all_gather(router_weight, ("dp", "fsdp"), axis=0, tiled=True),
+        jnp.concatenate(
+            lax.all_to_all(
+                jnp.stack([router_weight] * lax.axis_size(("dp", "fsdp"))), ("dp", "fsdp"), 0, 0
+            ),
+            axis=0,
+        ),
     )
     expert_full = (
         lax.all_gather(expert_gate, "fsdp", axis=1, tiled=True),

time: 1180 us -> 1120 us (0.949)
  waiting for transfers between devices: 901 us -> 842 us
    unnamed x16, waiting for transfers between devices: 69.8 us -> 4.48 us
    all_to_all x1, waiting for transfers between devices: 0.01 us -> 18.1 us  [shards(): lax.all_to_all(out_rows.reshape(recv_rows.shape), 'dp', split_axis=0, con...]
    all_gather x1, waiting for transfers between devices: 12 us -> 0.02 us  [shards(): lax.all_gather(expert_gate, 'fsdp', axis=1, tiled=True)]
  transfers between devices with their start and end apart: 19 -> 20, of which waited for: 16 -> 15; matrix products, arithmetic and copies ran while one was open for 6% -> 7% of each run, Pallas kernels for 0% -> 0%
where the time goes in v1:
time: 1120 us
  waiting for transfers between devices  842 us (75%)
  blocking collectives  151 us (13%)
  matrix products  51.4 us (5%)
  starting transfers between devices  24.9 us (2%)
  other arithmetic  18.5 us (2%)
  local copies, waits for them, and re-layouts  15.9 us (1%)
  between operations  14.8 us (1%)
    reduce_scatter x1, waiting for transfers between devices, shards(): lax.psum_scatter(grad_w_output, ('dp', 'fsdp'), scatter_dimension=0, tile...  143 us
    reduce_scatter x1, waiting for transfers between devices, shards(): lax.psum_scatter(grad_w_query, ('dp', 'fsdp'), scatter_dimension=0, tiled...  143 us
    reduce_scatter x1, waiting for transfers between devices, shards(): lax.psum_scatter(grad_w_key, ('dp', 'fsdp'), scatter_dimension=0, tiled=T...  140 us
    reduce_scatter x1, waiting for transfers between devices, shards(): lax.psum_scatter(grad_w_value, ('dp', 'fsdp'), scatter_dimension=0, tiled...  138 us
    unnamed x2, blocking collectives  82.6 us
    all_gather x1, blocking collectives, shards(): lax.all_gather(router_weight, ('dp', 'fsdp'), axis=0, tiled=True)  68.6 us
    all_gather x1, waiting for transfers between devices, shards(): lax.all_gather(query_weight, ('dp', 'fsdp'), axis=0, tiled=True)  56.5 us
    all_gather x1, waiting for transfers between devices, shards(): lax.all_gather(output_weight, ('dp', 'fsdp'), axis=0, tiled=True)  54.2 us
  transfers between devices with their start and end apart: 20, of which 15 were waited for; matrix products, arithmetic and copies ran while one was open for 7% of the time, Pallas kernels for 0%

profile of v1, /device:TPU:0, one launch (start us, length us, event | category | flops | bytes accessed | tf_op | source)
XLA Modules:
  0.0 1118.7 jit_solution(4562393542180636791)
XLA Ops:
  15.2 41.9 %all-reduce.5 = (bf16[1024]{0:T(1024)(128)(2,1)S(1)}, bf16[1024]{0:T(1024)(128)(2,1)S(1)}) all-reduce(bf16[1024]{0:T(1024)(128)(2,1)S(1)} %dynamic-update-slice, bf16[1024]{0:T(1024)(128)(2,1)S(1)} %dynamic-update-slice.1), channel_id=1, replica_groups=mesh['dp'=16,'fsdp'=2] {'dp','fsdp'}, use_global_device_ids=true, to_apply=%add | all-reduce | flops 2048 | bytes 8192
  59.3 8.2 all-gather.9.cloned.1.call-done
  67.5 1.7 convolution_convert_fusion.5
  69.3 54.0 %all-gather.11.cloned.1.call-done = bf16[1024,512]{1,0:T(8,128)(2,1)} async-done(((bf16[32,512]{1,0:T(8,128)(2,1)}), bf16[1024,512]{1,0:T(8,128)(2,1)}) %all-gather.11.cloned.1.call-update) | async-done | bytes 1048592 | tf_op jit(solution)/shard_map/all_gather | solution.py:144
  123.2 1.8 fusion.99
  125.1 56.5 %all-gather.13.cloned.1.call-done = bf16[1024,1024]{1,0:T(8,128)(2,1)} async-done(((bf16[32,1024]{1,0:T(8,128)(2,1)}), bf16[1024,1024]{1,0:T(8,128)(2,1)}) %all-gather.13.cloned.1.call-update) | async-done | bytes 2097168 | tf_op jit(solution)/shard_map/all_gather | solution.py:143
  181.6 2.6 fusion.97
  185.5 54.2 %all-gather.15.cloned.1.call-done = bf16[1024,1024]{1,0:T(8,128)(2,1)} async-done(((bf16[32,1024]{1,0:T(8,128)(2,1)}), bf16[1024,1024]{1,0:T(8,128)(2,1)}) %all-gather.15.cloned.1.call-update) | async-done | bytes 2097168 | tf_op jit(solution)/shard_map/all_gather | solution.py:146
  239.7 2.1 multiply_reduce_fusion.5
  244.0 4.5 all-to-all-start.1
  250.0 17.1 %all-to-all-done.1 = bf16[16,24,1024]{2,1,0:T(8,128)(2,1)S(1)} async-done(((bf16[16,24,1024]{2,1,0:T(8,128)(2,1)}), bf16[16,24,1024]{2,1,0:T(8,128)(2,1)S(1)}, u32[]{:S(2)}, u32[]{:S(2)}) %all-to-all-start.1) | async-done | bytes 786464 | tf_op jit(solution)/shard_map/all_to_all | solution.py:197
  267.2 4.4 all-to-all-start
  271.6 1.8 fusion.25
  273.4 10.9 all-gather.19.cloned.1.call-done
  284.3 2.7 multiply_convert_fusion.3
  287.0 20.2 %all-gather.21.cloned.1.call-done = bf16[1,512,1024]{2,1,0:T(8,128)(2,1)} async-done(((bf16[1,256,1024]{2,1,0:T(8,128)(2,1)}), bf16[1,512,1024]{2,1,0:T(8,128)(2,1)}) %all-gather.21.cloned.1.call-update) | async-done | bytes 1048592 | tf_op jit(solution)/shard_map/all_gather | solution.py:158
  307.2 2.7 convolution_convert_fusion.3
  309.9 5.6 all-to-all-start.2
  316.1 18.1 %all-to-all-done.2 = bf16[16,24,1024]{2,1,0:T(8,128)(2,1)S(1)} async-done(((bf16[16,24,1024]{2,1,0:T(8,128)(2,1)}), bf16[16,24,1024]{2,1,0:T(8,128)(2,1)S(1)}, u32[]{:S(2)}, u32[]{:S(2)}) %all-to-all-start.2) | async-done | bytes 786464 | tf_op jit(solution)/shard_map/all_to_all | solution.py:200
  335.9 5.4 all-to-all-start.3
  343.1 16.8 %all-to-all-done.3 = bf16[16,24,1024]{2,1,0:T(8,128)(2,1)S(1)} async-done(((bf16[16,24,1024]{2,1,0:T(8,128)(2,1)}), bf16[16,24,1024]{2,1,0:T(8,128)(2,1)S(1)}, u32[]{:S(2)}, u32[]{:S(2)}) %all-to-all-start.3) | async-done | bytes 786464 | tf_op jit(solution)/shard_map/all_to_all | solution.py:240
  360.0 2.8 multiply_convert_fusion.1
  363.5 1.7 fusion.2
  365.3 68.6 %all-gather = bf16[32,32,16]{1,2,0:T(8,128)(2,1)S(1)} all-gather(bf16[1,32,16]{1,2,0:T(8,128)(2,1)} %bitcast.170), channel_id=1, replica_groups=mesh['dp'=16,'fsdp'=2] {'dp','fsdp'}, dimensions={0}, use_global_device_ids=true | all-gather | bytes 33792 | tf_op jit(solution)/shard_map/all_gather | solution.py:221
  434.6 1.7 reshape.309
  436.3 1.7 fusion.3
  438.1 1.7 fusion.23
  441.3 4.4 all-to-all-start.4
  447.7 4.1 gather_fusion
  451.8 2.3 multiply_reduce_fusion
  454.1 1.7 fusion.4
  455.9 8.6 all-to-all-done.4
  469.2 2.1 convolution_bitcast_fusion.4
  471.4 1.9 fusion.93
  473.3 2.1 fusion.15
  475.5 1.8 fusion.91
  477.4 2.1 convolution_bitcast_fusion.1
  479.6 2.8 fusion.95
  483.4 2.7 fusion.56
  490.0 40.7 %all-reduce.4 = (f32[1024]{0:T(1024)S(1)}, f32[1024]{0:T(1024)S(1)}) all-reduce(f32[1024]{0:T(1024)S(1)} %get-tuple-element.14, f32[1024]{0:T(1024)S(1)} %copy-done.48), channel_id=2, replica_groups=mesh['dp'=16,'fsdp'=2] {'dp','fsdp'}, use_global_device_ids=true, to_apply=%region_17.18.clone | all-reduce | flops 2048 | bytes 16384
  532.8 2.1 convert_element_type.188
  535.0 2.1 convert_element_type.191
  537.1 9.2 reduce-scatter.23.cloned.1.call-done
  546.4 2.1 convert_element_type.194
  548.5 139.7 %reduce-scatter.13.cloned.1.call-done = f32[32,512]{1,0:T(8,128)} async-done(((f32[1024,512]{1,0:T(8,128)}), f32[32,512]{1,0:T(8,128)}) %reduce-scatter.13.cloned.1.call-update) | async-done | bytes 65552 | tf_op jit(solution)/shard_map/reduce_scatter | solution.py:306
  688.2 138.0 %reduce-scatter.15.cloned.1.call-done = f32[32,512]{1,0:T(8,128)} async-done(((f32[1024,512]{1,0:T(8,128)}), f32[32,512]{1,0:T(8,128)}) %reduce-scatter.15.cloned.1.call-update) | async-done | bytes 65552 | tf_op jit(solution)/shard_map/reduce_scatter | solution.py:307
  826.2 142.7 %reduce-scatter.11.cloned.1.call-done = f32[32,1024]{1,0:T(8,128)} async-done(((f32[1024,1024]{1,0:T(8,128)}), f32[32,1024]{1,0:T(8,128)}) %reduce-scatter.11.cloned.1.call-update) | async-done | bytes 131088 | tf_op jit(solution)/shard_map/reduce_scatter | solution.py:305
  969.0 143.2 %reduce-scatter.17.cloned.1.call-done = f32[32,1024]{1,0:T(8,128)} async-done(((f32[1024,1024]{1,0:T(8,128)}), f32[32,1024]{1,0:T(8,128)}) %reduce-scatter.17.cloned.1.call-update) | async-done | bytes 131088 | tf_op jit(solution)/shard_map/reduce_scatter | solution.py:308
  (212 shorter events, 35.9 us)
Async XLA Ops:
  7.2 116.1 %copy-start = (bf16[128,1024]{1,0:T(8,128)(2,1)S(1)}, bf16[128,1024]{1,0:T(8,128)(2,1)}, u32[]{:S(2)}) copy-start(bf16[128,1024]{1,0:T(8,128)(2,1)} %param.14) | copy-start | bytes 786436
  7.2 60.3 %all-gather.9.cloned.1.call-start = ((), (), s32[]{:S(2)}) async-start(), calls=%async_computation.13 | async-start | bytes 1081344 | tf_op jit(solution)/shard_map/all_gather | solution.py:145
  7.9 115.3 %all-gather.11.cloned.1.call-start = ((), (), s32[]{:S(2)}) async-start(), calls=%async_computation.14 | async-start | bytes 1081344 | tf_op jit(solution)/shard_map/all_gather | solution.py:144
  8.7 172.9 %all-gather.13.cloned.1.call-start = ((), (), s32[]{:S(2)}) async-start(), calls=%async_computation.15 | async-start | bytes 2162688 | tf_op jit(solution)/shard_map/all_gather | solution.py:143
  9.4 230.3 %all-gather.15.cloned.1.call-start = ((), (), s32[]{:S(2)}) async-start(), calls=%async_computation.16 | async-start | bytes 2162688 | tf_op jit(solution)/shard_map/all_gather | solution.py:146
  10.0 261.6 %all-gather.17.cloned.1.call-start = ((), (), s32[]{:S(2)}) async-start(), calls=%async_computation.17 | async-start | bytes 1572864 | tf_op jit(solution)/shard_map/all_gather | solution.py:156
  10.6 273.7 %all-gather.19.cloned.1.call-start = ((), (), s32[]{:S(2)}) async-start(), calls=%async_computation.18 | async-start | bytes 1572864 | tf_op jit(solution)/shard_map/all_gather | solution.py:157
  11.8 329.5 %copy-start.54 = (f32[128]{0:T(128)}, f32[128]{0:T(128)S(1)}, u32[]{:S(2)}) copy-start(f32[128]{0:T(128)S(1)} %compare_convert_fusion) | copy-start | bytes 1540
  13.5 171.5 %copy-start.50 = (pred[128,128]{0,1:T(8,128)(4,1)}, pred[128,128]{0,1:T(8,128)(4,1)S(1)}, u32[]{:S(2)}) copy-start(pred[128,128]{0,1:T(8,128)(4,1)S(1)} %compare_and_fusion.1) | copy-start | bytes 49156
  57.1 127.0 %copy-start.29 = (f32[1024]{0:T(1024)}, f32[1024]{0:T(1024)S(1)}, u32[]{:S(2)}) copy-start(f32[1024]{0:T(1024)S(1)} %convert_element_type.150) | copy-start | bytes 12292
  58.2 126.0 %copy-start.46 = (f32[128]{0:T(128)}, f32[128]{0:T(128)S(1)}, u32[]{:S(2)}) copy-start(f32[128]{0:T(128)S(1)} %add_rsqrt_fusion.1) | copy-start | bytes 1540
  58.2 183.6 %copy-start.40 = (f32[1024]{0:T(1024)}, f32[1024]{0:T(1024)S(1)}, u32[]{:S(2)}) copy-start(f32[1024]{0:T(1024)S(1)} %convert_element_type.161) | copy-start | bytes 12292
  59.1 125.1 %copy-start.25 = (f32[128,32]{0,1:T(8,128)}, f32[128,32]{0,1:T(8,128)S(1)}, u32[]{:S(2)}) copy-start(f32[128,32]{0,1:T(8,128)S(1)} %get-tuple-element.41) | copy-start | bytes 49156
  59.2 275.4 %copy-start.38 = (f32[16,128]{1,0:T(8,128)}, f32[16,128]{1,0:T(8,128)S(1)}, u32[]{:S(2)}) copy-start(f32[16,128]{1,0:T(8,128)S(1)} %get-tuple-element.42) | copy-start | bytes 24580
  59.2 282.1 %copy-start.31 = (f32[128,16]{0,1:T(8,128)}, f32[128,16]{0,1:T(8,128)S(1)}, u32[]{:S(2)}) copy-start(f32[128,16]{0,1:T(8,128)S(1)} %get-tuple-element.43) | copy-start | bytes 24580
  69.3 115.7 %copy-start.19 = (bf16[128,512]{0,1:T(8,128)(2,1)}, bf16[128,512]{0,1:T(8,128)(2,1)S(1)}, u32[]{:S(2)}) copy-start(bf16[128,512]{0,1:T(8,128)(2,1)S(1)} %copy.86) | copy-start | bytes 393220
  125.1 59.5 %copy-start.33 = (bf16[128,8,32]{0,2,1:T(8,128)(2,1)}, bf16[128,8,32]{0,2,1:T(8,128)(2,1)S(1)}, u32[]{:S(2)}) copy-start(bf16[128,8,32]{0,2,1:T(8,128)(2,1)S(1)} %get-tuple-element.36) | copy-start | bytes 196612
  125.1 59.5 %copy-start.35 = (bf16[128,8,32]{0,2,1:T(8,128)(2,1)}, bf16[128,8,32]{0,2,1:T(8,128)(2,1)S(1)}, u32[]{:S(2)}) copy-start(bf16[128,8,32]{0,2,1:T(8,128)(2,1)S(1)} %get-tuple-element.37) | copy-start | bytes 196612
  185.0 56.8 %copy-start.13 = (f32[8,2,128,128]{2,3,1,0:T(8,128)}, f32[8,2,128,128]{2,3,1,0:T(8,128)S(1)}, u32[]{:S(2)}) copy-start(f32[8,2,128,128]{2,3,1,0:T(8,128)S(1)} %fusion.12) | copy-start | bytes 3145732
  185.5 58.5 %copy-start.16 = (bf16[8,64,2,128]{3,1,2,0:T(8,128)(2,1)}, bf16[8,64,2,128]{3,1,2,0:T(8,128)(2,1)S(1)}, u32[]{:S(2)}) copy-start(bf16[8,64,2,128]{3,1,2,0:T(8,128)(2,1)S(1)} %fusion.14) | copy-start | bytes 786436
  241.8 7.4 copy-start.49
  244.0 23.2 %all-to-all-start.1 = ((bf16[16,24,1024]{2,1,0:T(8,128)(2,1)}), bf16[16,24,1024]{2,1,0:T(8,128)(2,1)S(1)}, u32[]{:S(2)}, u32[]{:S(2)}) async-start(bf16[16,24,1024]{2,1,0:T(8,128)(2,1)} %convolution_convert_fusion.4), calls=%async_computation.1 | async-start | bytes 1572864 | tf_op jit(solution)/shard_map/all_to_all | solution.py:197
  248.5 58.7 %all-gather.21.cloned.1.call-start = ((), (), s32[]{:S(2)}) async-start(), calls=%async_computation.19 | async-start | bytes 1572864 | tf_op jit(solution)/shard_map/all_gather | solution.py:158
  267.2 42.8 %all-to-all-start = ((bf16[32,2,256]{2,1,0:T(2,128)(2,1)}), bf16[32,2,256]{2,1,0:T(2,128)(2,1)S(1)}, u32[]{:S(2)}, u32[]{:S(2)}) async-start(bf16[32,2,256]{2,1,0:T(2,128)(2,1)} %reshape.319), calls=%async_computation | async-start | bytes 65536 | tf_op jit(solution)/shard_map/all_to_all | solution.py:149
  273.3 13.6 %copy-start.18 = (f32[384,512]{1,0:T(8,128)}, f32[384,512]{1,0:T(8,128)S(1)}, u32[]{:S(2)}) copy-start(f32[384,512]{1,0:T(8,128)S(1)} %fusion.25) | copy-start | bytes 2359300
  287.0 22.9 %copy-start.27 = (bf16[384,512]{1,0:T(8,128)(2,1)}, bf16[384,512]{1,0:T(8,128)(2,1)S(1)}, u32[]{:S(2)}) copy-start(bf16[384,512]{1,0:T(8,128)(2,1)S(1)} %get-tuple-element.46) | copy-start | bytes 1179652
  307.2 27.1 %copy-start.12 = (bf16[128,1024]{1,0:T(8,128)(2,1)S(1)}, bf16[128,1024]{1,0:T(8,128)(2,1)}, u32[]{:S(2)}) copy-start(bf16[128,1024]{1,0:T(8,128)(2,1)} %param.17) | copy-start | bytes 786436
  309.9 24.3 %all-to-all-start.2 = ((bf16[16,24,1024]{2,1,0:T(8,128)(2,1)}), bf16[16,24,1024]{2,1,0:T(8,128)(2,1)S(1)}, u32[]{:S(2)}, u32[]{:S(2)}) async-start(bf16[16,24,1024]{2,1,0:T(8,128)(2,1)} %bitcast.17), calls=%async_computation.2 | async-start | bytes 1572864 | tf_op jit(solution)/shard_map/all_to_all | solution.py:200
  335.9 24.1 %all-to-all-start.3 = ((bf16[16,24,1024]{2,1,0:T(8,128)(2,1)}), bf16[16,24,1024]{2,1,0:T(8,128)(2,1)S(1)}, u32[]{:S(2)}, u32[]{:S(2)}) async-start(bf16[16,24,1024]{2,1,0:T(8,128)(2,1)} %multiply_convert_fusion), calls=%async_computation.3 | async-start | bytes 1572864 | tf_op jit(solution)/shard_map/all_to_all | solution.py:240
  341.3 144.8 %reduce-scatter.25.cloned.1.call-start = ((), (), s32[]{:S(2)}) async-start(), calls=%async_computation.27 | async-start | bytes 540672
  342.0 18.0 %copy-start.42 = (bf16[128,16]{0,1:T(8,128)(2,1)}, bf16[128,16]{0,1:T(8,128)(2,1)S(1)}, u32[]{:S(2)}) copy-start(bf16[128,16]{0,1:T(8,128)(2,1)S(1)} %get-tuple-element.38) | copy-start | bytes 12292
  343.1 189.8 %reduce-scatter.19.cloned.1.call-start = ((), (), s32[]{:S(2)}) async-start(), calls=%async_computation.24 | async-start | bytes 1572864 | tf_op jit(solution)/shard_map/reduce_scatter | solution.py:313
  365.3 72.8 %copy-start.5 = (bf16[1,1024,512]{2,1,0:T(8,128)(2,1)S(1)}, bf16[1,1024,512]{2,1,0:T(8,128)(2,1)}, u32[]{:S(2)}) copy-start(bf16[1,1024,512]{2,1,0:T(8,128)(2,1)} %all-gather.17.cloned.1.call-done) | copy-start | bytes 3145732
  365.3 169.7 %reduce-scatter.21.cloned.1.call-start = ((), (), s32[]{:S(2)}) async-start(), calls=%async_computation.25 | async-start | bytes 1572864 | tf_op jit(solution)/shard_map/reduce_scatter | solution.py:316
  439.8 6.1 copy-start.14
  441.3 23.1 %all-to-all-start.4 = ((bf16[16,24,1024]{2,1,0:T(8,128)(2,1)}), bf16[16,24,1024]{2,1,0:T(8,128)(2,1)}, u32[]{:S(2)}, u32[]{:S(2)}) async-start(bf16[16,24,1024]{2,1,0:T(8,128)(2,1)} %bitcast.24), calls=%async_computation.4 | async-start | bytes 1572864 | tf_op jit(solution)/shard_map/all_to_all | solution.py:244
  445.8 100.6 %reduce-scatter.23.cloned.1.call-start = ((), (), s32[]{:S(2)}) async-start(), calls=%async_computation.26 | async-start | bytes 1572864 | tf_op jit(solution)/shard_map/reduce_scatter | solution.py:319
  454.1 10.4 copy-start.39
  454.1 11.9 %copy-start.4 = (f32[128,1024]{1,0:T(8,128)S(1)}, f32[128,1024]{1,0:T(8,128)}, u32[]{:S(2)}) copy-start(f32[128,1024]{1,0:T(8,128)} %copy-done.3) | copy-start | bytes 1572868
  454.1 11.9 %copy-start.37 = (bf16[1024,16]{0,1:T(8,128)(2,1)S(1)}, bf16[1024,16]{0,1:T(8,128)(2,1)}, u32[]{:S(2)}) copy-start(bf16[1024,16]{0,1:T(8,128)(2,1)} %reshape.309) | copy-start | bytes 98308
  454.1 11.9 %copy-start.41 = (f32[1024]{0:T(1024)S(1)}, f32[1024]{0:T(1024)}, u32[]{:S(2)}) copy-start(f32[1024]{0:T(1024)} %copy-done.40) | copy-start | bytes 12292
  454.1 11.9 %copy-start.43 = (bf16[128,16]{0,1:T(8,128)(2,1)S(1)}, bf16[128,16]{0,1:T(8,128)(2,1)}, u32[]{:S(2)}) copy-start(bf16[128,16]{0,1:T(8,128)(2,1)} %copy-done.42) | copy-start | bytes 12292
  454.1 11.9 %copy-start.53 = (f32[128]{0:T(128)S(1)}, f32[128]{0:T(128)}, u32[]{:S(2)}) copy-start(f32[128]{0:T(128)} %copy-done.52) | copy-start | bytes 1540
  455.8 11.1 copy-start.10
  455.9 232.4 %reduce-scatter.13.cloned.1.call-start = ((), (), s32[]{:S(2)}) async-start(), calls=%async_computation.21 | async-start | bytes 2162688 | tf_op jit(solution)/shard_map/reduce_scatter | solution.py:306
  473.3 352.9 %reduce-scatter.15.cloned.1.call-start = ((), (), s32[]{:S(2)}) async-start(), calls=%async_computation.22 | async-start | bytes 2162688 | tf_op jit(solution)/shard_map/reduce_scatter | solution.py:307
  477.3 491.6 %reduce-scatter.11.cloned.1.call-start = ((), (), s32[]{:S(2)}) async-start(), calls=%async_computation.20 | async-start | bytes 4325376 | tf_op jit(solution)/shard_map/reduce_scatter | solution.py:305
  482.4 629.7 %reduce-scatter.17.cloned.1.call-start = ((), (), s32[]{:S(2)}) async-start(), calls=%async_computation.23 | async-start | bytes 4325376 | tf_op jit(solution)/shard_map/reduce_scatter | solution.py:308
  (28 other events, 62.5 us)
Sparse Core Ops, SparseCore 0:
  10.9 56.5 all-gather.8
  70.4 52.8 all-gather.10
  126.2 55.3 all-gather.12
  184.4 55.1 all-gather.14
  241.1 20.1 all-gather.16
  262.6 21.6 all-gather.18
  285.8 21.2 all-gather.20
  344.4 136.7 reduce-scatter.24
  484.0 16.9 reduce-scatter.18
  503.1 20.5 reduce-scatter.20
  525.9 20.4 reduce-scatter.22
  549.1 139.1 reduce-scatter.12
  691.1 135.1 reduce-scatter.14
  829.0 139.9 reduce-scatter.10
  971.6 140.4 reduce-scatter.16
